TPU v7x, 32 devices: a whole 2x2x4 slice. The times are simulated.
32 devices in a mesh: row: 4 (over z), col: 8 (over y, x, core).
Axes of the slice: x: 2, y: 2, z: 4, core: 2. Of those that a mesh axis runs over, the one named last changes fastest.
Arguments:
- src_feats: bfloat16 [65536, 128], P(('row', 'col')), may hold values from -32 to 32
- dst_feats: bfloat16 [2048, 128], P(('row', 'col')), may hold values from -6 to 6
- proj_weight: bfloat16 [128, 256], replicated, may hold values from -0.5 to 0.5
- attn_src: float32 [4, 64], replicated, may hold values from -1.5 to 1.5
- attn_dst: float32 [4, 64], replicated, may hold values from -2 to 2
- tile_dst: int32 [4, 2048], P('row', 'col'), may hold values from 0 to 3, as said below
- tile_src: int32 [4, 2048], P('row', 'col'), may hold values from 0 to 63
- tile_live: int32 [4, 8], P('row', 'col'), may hold values from 64 to 256, as said below
- tile_mask: int32 [4, 2048, 2048], P('row', 'col'), may hold values from 0 to 255, as said below
Outputs:
- attended: bfloat16 [2048, 256], P(('row', 'col'))
Inputs may be any that keep to these rules, and one draw needn't show every extreme that they name: The pairs (tile_dst, tile_src) of one device's 256 slots are distinct. `tile_live`: in every draw some device has all 256 slots live. `tile_mask`: each word holds the edge bits of 8 consecutive source columns of one destination row of a tile in its lowest 8 bits; slots at or past a device's live count carry arbitrary bits.
All inputs are finite; a program needn't handle non-finite values.
Results may differ from a plain program's by a relative error of at most 0.015.
Values may be sent and summed in bfloat16 or wider, within the bound.
A program may use at most 64 MiB of HBM per device.

v0:
```python
import jax
import jax.numpy as jnp
from jax import lax
from jax.sharding import PartitionSpec as P

HEADS = 4
HEAD_DIM = 64
DST_DEV = 512
SRC_COL = 8192


neg_fill = -1e30


def combined_all(shard, axis, combine):
    everything = jax.tree.map(
        lambda part, kind: lax.all_gather(part.astype(kind), axis),
        shard,
        (jnp.bfloat16, jnp.bfloat16, jnp.bfloat16),
    )

    def take(k):
        return jax.tree.map(lambda part, own: part[k].astype(own.dtype), everything, shard)

    return lax.fori_loop(
        1, lax.axis_size(axis), lambda k, so_far: combine(so_far, take(k)), take(0)
    )


def leaky_relu(values):
    return jnp.where(values >= 0, values, 0.2 * values)


def head_scores(hidden, attention):
    row_count = hidden.shape[0]
    return jnp.sum(
        hidden.astype(jnp.float32).reshape(row_count, HEADS, HEAD_DIM) * attention[None], axis=2
    )


def merge_parts(former, latter):
    top_max = jnp.maximum(former[0], latter[0])
    former_scale = jnp.exp(former[0] - top_max)
    latter_scale = jnp.exp(latter[0] - top_max)
    den_sum = former[1] * former_scale + latter[1] * latter_scale
    row_count = top_max.shape[0]
    num_sum = (
        former[2].reshape(row_count, HEADS, HEAD_DIM) * former_scale[:, :, None]
        + latter[2].reshape(row_count, HEADS, HEAD_DIM) * latter_scale[:, :, None]
    )
    return (top_max, den_sum, num_sum.reshape(row_count, HEADS * HEAD_DIM))


def body(
    src_feats, dst_feats, proj_weight, attn_src, attn_dst, tile_dst, tile_src, tile_live, tile_mask
):
    hidden_units = HEADS * HEAD_DIM
    blocks = DST_DEV // 128
    src_blocks = SRC_COL // 128
    tiles_turn = 8
    own_hidden = jnp.dot(dst_feats, proj_weight, preferred_element_type=jnp.float32).astype(
        jnp.bfloat16
    )
    own_dest = head_scores(own_hidden, attn_dst)
    own_source = head_scores(own_hidden, attn_src)
    block_dest = lax.all_gather(own_dest.T, "col", axis=1, tiled=True)
    slab_hidden = jnp.dot(
        lax.all_gather(src_feats, "row", axis=0, tiled=True),
        proj_weight,
        preferred_element_type=jnp.float32,
    ).astype(jnp.bfloat16)
    slab_score = head_scores(slab_hidden, attn_src)
    dest_table = block_dest.reshape(HEADS, blocks, 128).transpose(1, 0, 2)
    source_table = slab_score.reshape(src_blocks, 128, HEADS).transpose(0, 2, 1)
    value_table = slab_hidden.reshape(src_blocks, 128, hidden_units)
    dest_slots = tile_dst[0]
    source_slots = tile_src[0]
    packed_all = tile_mask[0]
    live_count = tile_live[0, 0]
    shifts = jnp.arange(8, dtype=jnp.int32)
    block_iota = jnp.arange(blocks, dtype=jnp.int32)
    source_iota = jnp.arange(src_blocks, dtype=jnp.int32)
    turn_iota = jnp.arange(tiles_turn, dtype=jnp.int32)

    def one_turn(turn_index, state_in):
        run_max, run_den, run_num = state_in
        offset = turn_index * tiles_turn
        turn_dest = lax.dynamic_slice_in_dim(dest_slots, offset, tiles_turn)
        turn_source = lax.dynamic_slice_in_dim(source_slots, offset, tiles_turn)
        turn_packed = lax.dynamic_slice_in_dim(packed_all, offset, tiles_turn, 0)
        layered = turn_packed.reshape(tiles_turn, 128, 16, 1) >> shifts & 1
        present = (layered.reshape(tiles_turn, 128, 128) == 1) & (offset + turn_iota < live_count)[
            :, None, None
        ]
        present = present[:, None]
        member = (turn_dest[:, None] == block_iota[None, :])[:, :, None, None]
        source_member = (turn_source[:, None] == source_iota[None, :])[:, :, None, None]
        dest_part = jnp.sum(jnp.where(member, dest_table[None], 0.0), axis=1)
        source_part = jnp.sum(jnp.where(source_member, source_table[None], 0.0), axis=1)
        values = jnp.take(value_table, turn_source, axis=0)
        scores = leaky_relu(dest_part[:, :, :, None] + source_part[:, :, None, :])
        tile_top = jnp.max(jnp.where(present, scores, neg_fill), axis=3)
        turn_top = jnp.max(jnp.where(member, tile_top[:, None], neg_fill), axis=0)
        new_max = jnp.maximum(run_max, turn_top)
        keep_scale = jnp.exp(run_max - new_max)
        tile_shift = jnp.sum(jnp.where(member, new_max[None], 0.0), axis=1)
        weights = jnp.where(present, jnp.exp(scores - tile_shift[:, :, :, None]), 0.0)
        den_terms = jnp.sum(jnp.where(member, jnp.sum(weights, axis=3)[:, None], 0.0), axis=0)
        products = jnp.einsum(
            "ghij,gjhd->gihd",
            weights.astype(jnp.bfloat16),
            values.reshape(tiles_turn, 128, HEADS, HEAD_DIM),
            preferred_element_type=jnp.float32,
        )
        onehot = (turn_dest[:, None] == block_iota[None, :]).astype(jnp.float32)
        num_terms = jnp.einsum(
            "gb,gir->bir",
            onehot,
            products.reshape(tiles_turn, 128, hidden_units),
            precision=lax.Precision.HIGHEST,
        )
        scaled = (
            run_num.reshape(blocks, 128, HEADS, HEAD_DIM)
            * keep_scale.transpose(0, 2, 1)[:, :, :, None]
        )
        return (
            new_max,
            run_den * keep_scale + den_terms,
            scaled.reshape(blocks, 128, hidden_units) + num_terms,
        )

    turn_count = (live_count + tiles_turn - 1) // tiles_turn
    initial = (
        jnp.full((blocks, HEADS, 128), neg_fill, jnp.float32),
        jnp.zeros((blocks, HEADS, 128), jnp.float32),
        jnp.zeros((blocks, 128, hidden_units), jnp.float32),
    )
    run_max, run_den, run_num = lax.fori_loop(0, turn_count, one_turn, initial)
    part_max = run_max.transpose(0, 2, 1).reshape(DST_DEV, HEADS)
    part_den = run_den.transpose(0, 2, 1).reshape(DST_DEV, HEADS)
    part_num = run_num.reshape(DST_DEV, hidden_units)
    own_rows = own_hidden.shape[0]
    first_row = lax.axis_index("col") * own_rows
    row_top, den_all, num_all = combined_all((part_max, part_den, part_num), "col", merge_parts)
    top_own = lax.dynamic_slice_in_dim(row_top, first_row, own_rows, 0)
    den_own = lax.dynamic_slice_in_dim(den_all, first_row, own_rows, 0)
    num_own = lax.dynamic_slice_in_dim(num_all, first_row, own_rows, 0)
    self_score = leaky_relu(own_dest + own_source)
    final_max = jnp.maximum(top_own, self_score)
    back_scale = jnp.exp(top_own - final_max)
    self_weight = jnp.exp(self_score - final_max)
    den_total = den_own * back_scale + self_weight
    rounded_self = lax.optimization_barrier(self_weight.astype(jnp.bfloat16)).astype(jnp.float32)
    num_total = num_own.reshape(own_rows, HEADS, HEAD_DIM) * back_scale[:, :, None] + rounded_self[
        :, :, None
    ] * own_hidden.astype(jnp.float32).reshape(own_rows, HEADS, HEAD_DIM)
    return (num_total / den_total[:, :, None]).reshape(own_rows, hidden_units).astype(jnp.bfloat16)


def solution(mesh):
    placed = (
        P(("row", "col"), None),
        P(("row", "col"), None),
        P(),
        P(),
        P(),
        P("row", "col"),
        P("row", "col"),
        P("row", "col"),
        P("row", "col", None),
    )
    return jax.shard_map(
        body, mesh=mesh, in_specs=placed, out_specs=P(("row", "col"), None), check_vma=False
    )
```

profile of v0, /device:TPU:0, one launch (start us, length us, event | category | flops | bytes accessed | tf_op | source)
XLA Modules:
  0.0 575.8 jit_solution(5491627048766676860)
XLA Ops:
  9.9 10.4 %all-gather = f32[8,64,4]{1,2,0:T(4,128)S(1)} all-gather(f32[1,64,4]{1,2,0:T(4,128)S(1)} %copy.114), channel_id=1, replica_groups=mesh['row'=4,'col'=8] {'col'}, dimensions={0}, use_global_device_ids=true | all-gather | bytes 9216 | tf_op jit(solution)/shard_map/all_gather | solution.py:66
  20.5 36.9 %all-gather.4.cloned.1.call-done = bf16[8192,128]{1,0:T(8,128)(2,1)} async-done(((bf16[2048,128]{1,0:T(8,128)(2,1)}), bf16[8192,128]{1,0:T(8,128)(2,1)}) %all-gather.4.cloned.1.call-update) | async-done | bytes 2097168 | tf_op jit(solution)/shard_map/all_gather | solution.py:68
  57.3 4.8 convolution_convert_fusion
  62.1 7.1 %copy.116 = f32[8192,256]{0,1:T(8,128)} copy(bf16[8192,256]{1,0:T(8,128)(2,1)} %convolution_convert_fusion) | data formatting | bytes 12582912 | tf_op jit(solution)/shard_map/reshape | solution.py:37
  69.2 4.4 multiply_reduce_fusion
  73.8 198.8 %while.37 = (s32[]{:T(128)}, f32[4,4,128]{2,1,0:T(4,128)S(1)}, f32[4,4,128]{2,1,0:T(4,128)S(1)}, f32[4,128,256]{2,0,1:T(4,128)S(1)}, s32[]{:T(128)}, /*index=5*/...) while((s32[]{:T(128)}, f32[4,4,128]{2,1,0:T(4,128)S(1)}, ...), condition=%wide.region_10.11_spmd.clone.clone, body=%wide.region_2.10_spmd.clone.clone.sunk | while | flops 91868832 | bytes 11853559 | solution.py:138
  81.4 2.8 fusion.63
  95.6 2.8 fusion.63
  109.8 2.8 fusion.63
  124.0 2.8 fusion.63
  138.2 2.8 fusion.63
  152.4 2.8 fusion.63
  166.6 2.8 fusion.63
  180.8 2.8 fusion.63
  195.0 2.8 fusion.63
  209.2 2.8 fusion.63
  223.4 2.8 fusion.63
  237.6 2.8 fusion.63
  251.8 2.8 fusion.63
  266.0 2.8 fusion.63
  273.6 7.0 %all_gather.21 = bf16[8,512,4]{1,2,0:T(4,128)(2,1)S(1)} all-gather(bf16[1,512,4]{1,2,0:T(4,128)(2,1)S(1)} %convert_bitcast_fusion), channel_id=1, replica_groups=mesh['row'=4,'col'=8] {'col'}, dimensions={0}, use_global_device_ids=true | all-gather | bytes 36864 | tf_op jit(solution)/shard_map/all_gather | solution.py:17
  280.6 10.2 %all_gather.20 = bf16[8,512,4]{1,2,0:T(4,128)(2,1)S(1)} all-gather(bf16[1,512,4]{1,2,0:T(4,128)(2,1)S(1)} %convert_bitcast_fusion.1), channel_id=1, replica_groups=mesh['row'=4,'col'=8] {'col'}, dimensions={0}, use_global_device_ids=true | all-gather | bytes 36864 | tf_op jit(solution)/shard_map/all_gather | solution.py:17
  290.8 264.9 %all-gather.6.cloned.1.call-done = bf16[8,512,256]{2,1,0:T(8,128)(2,1)} async-done(((bf16[1,512,256]{2,1,0:T(8,128)(2,1)}), bf16[8,512,256]{2,1,0:T(8,128)(2,1)}) %all-gather.6.cloned.1.call-update) | async-done | bytes 2097168 | tf_op jit(solution)/shard_map/all_gather | solution.py:17
  556.9 10.0 %while.36 = (s32[]{:T(128)}, f32[512,4]{0,1:T(4,128)S(1)}, f32[512,4]{0,1:T(4,128)S(1)}, f32[512,256]{0,1:T(8,128)S(1)}, bf16[8,512,4]{1,2,0:T(4,128)(2,1)S(1)},...) while((s32[]{:T(128)}, f32[512,4]{0,1:T(4,128)S(1)}, ...), condition=%wide.region_12.13_spmd, body=%wide.region_11.12_spmd.sunk | while | flops 540677 | bytes 2433175 | solution.py:25
  (535 shorter events, 174.4 us)
Async XLA Ops:
  6.5 1.4 copy-start
  6.5 50.8 %all-gather.4.cloned.1.call-start = ((), (), s32[]{:S(2)}) async-start(), calls=%async_computation | async-start | bytes 2621440 | tf_op jit(solution)/shard_map/all_gather | solution.py:68
  7.3 548.4 %all-gather.6.cloned.1.call-start = ((), (), s32[]{:S(2)}) async-start(), calls=%async_computation.1 | async-start | bytes 2359296 | tf_op jit(solution)/shard_map/all_gather | solution.py:17
  62.1 7.1 %copy-start.1 = (f32[4,64]{1,0:T(4,128)S(1)}, f32[4,64]{1,0:T(4,128)}, u32[]{:S(2)}) copy-start(f32[4,64]{1,0:T(4,128)} %param.16) | copy-start | bytes 3076
  69.2 4.6 copy-start.2
  69.2 4.6 copy-start.3
Sparse Core Ops, SparseCore 0:
  8.9 48.3 all-gather.3
  273.5 282.0 all-gather.5
where the time goes:
time: 579 us; the launch traced here: 576 us
  waiting for transfers between devices  302 us (52%)
  local copies, waits for them, and re-layouts  94.2 us (16%)
  other arithmetic  76.6 us (13%)
  matrix products  58.1 us (10%)
  blocking collectives  27.6 us (5%)
  between operations  14.2 us (2%)
    all_gather x1, waiting for transfers between devices, combined_all(): lax.all_gather(part.astype(kind), axis)  265 us
    gather x28, local copies, waits for them, and re-layouts, one_turn(): values = jnp.take(value_table, turn_source, axis=0)  42.6 us
    dot_general x14, matrix products, one_turn(): jnp.einsum('ghij,gjhd->gihd', weights.astype(jnp.bfloat16), values.reshap...  39 us
    all_gather x1, waiting for transfers between devices, body(): lax.all_gather(src_feats, 'row', axis=0, tiled=True)  36.9 us
    reduce_sum x14, other arithmetic, one_turn(): jnp.sum(weights, axis=3)[:, None]  27.1 us
    reduce_max x14, other arithmetic, one_turn(): tile_top = jnp.max(jnp.where(present, scores, neg_fill), axis=3)  18.3 us
    all_gather x2, blocking collectives, combined_all(): lax.all_gather(part.astype(kind), axis)  17.2 us
    dot_general x14, matrix products, one_turn(): jnp.einsum('gb,gir->bir', onehot, products.reshape(tiles_turn, 128, hidde...  13.4 us
  transfers between devices with their start and end apart: 2, of which 2 were waited for; matrix products, arithmetic and copies ran while one was open for 0% of the time, Pallas kernels for 0%

commit v1 on v0

v1 whole, which is shorter than its diff:
```python
import functools
import jax
import jax.numpy as jnp
from jax import lax
from jax.experimental import pallas as pl
from jax.experimental.pallas import tpu as pltpu
from jax.sharding import PartitionSpec as P

BF = jnp.bfloat16
F32 = jnp.float32
NEG = -1e30
SPAN = 40.0
GROUP = 4


def leaky(x):
    return jnp.maximum(x, 0.2 * x)


def split3(x):
    first = x.astype(BF)
    rest = x - first.astype(F32)
    second = rest.astype(BF)
    third = (rest - second.astype(F32)).astype(BF)
    return first, second, third


def dot(a, b):
    return jnp.dot(a, b, preferred_element_type=F32)


def dot_exact(a, b32):
    return sum(dot(a, part) for part in split3(b32))


def order_matrix(rows, inverse):
    per = rows // 8
    a = lax.broadcasted_iota(jnp.int32, (rows, rows), 0)
    b = lax.broadcasted_iota(jnp.int32, (rows, rows), 1)
    if inverse:
        a, b = b, a
    return jnp.where(b == (a % per) * 8 + a // per, 1.0, 0.0).astype(BF)


def main_kernel(
    heads, inv_ref, feats_ref, dst_ref, weight_ref, asrc_ref, adst_ref, expand_ref, packed_ref,
    out_ref, mask_ref, value_ref, score_ref, factor_ref, fa_ref, fc_ref, d_ref, m_ref, w_ref,
    acc_ref, sems
):
    units = weight_ref.shape[1]
    slabs = feats_ref.shape[0]
    nsb = slabs // 128
    nd = dst_ref.shape[0]
    blocks = nd // 128
    slots = packed_ref.shape[0]
    pitch = mask_ref.shape[0] // 16
    half = units // heads
    copies = [
        pltpu.make_async_copy(
            packed_ref.at[:, pl.ds(u * 128, 128)], mask_ref.at[pl.ds(u * pitch, slots), :], sems.at[u]
        )
        for u in range(16)
    ]
    for copy in copies:
        copy.start()
    for u in range(16):
        mask_ref[u * pitch + slots : (u + 1) * pitch, :] = jnp.zeros((pitch - slots, 128), jnp.int32)

    lane = lax.broadcasted_iota(jnp.int32, (1, 128), 1)
    weight = weight_ref[...]
    arows = asrc_ref[...]
    a_parts = jnp.concatenate([p.astype(F32) for p in split3(arows)] + [jnp.zeros_like(arows)], 0).astype(BF)
    chunk = 512

    def project(k, carry):
        rows = pl.ds(pl.multiple_of(k * chunk, chunk), chunk)
        hidden = dot(feats_ref[rows, :], weight).astype(BF)
        parts = lax.dot_general(
            a_parts, hidden, (((1,), (1,)), ((), ())), preferred_element_type=F32
        )
        score_ref[:, rows] = parts[0:8] + parts[8:16] + parts[16:24]
        for h in range(heads):
            tile = hidden[:, (h // 2) * 128 : (h // 2) * 128 + 128]
            own = (lane >= half) if h % 2 else (lane < half)
            value_ref[rows, h * 128 : h * 128 + 128] = jnp.where(own, tile.astype(F32), 1.0).astype(BF)
        return carry

    lax.fori_loop(0, slabs // chunk, project, 0)
    scores = score_ref[0:heads, :]
    top = jnp.max(scores, axis=1, keepdims=True)
    low = jnp.min(scores, axis=1, keepdims=True)
    wide = jnp.max(top - low) > SPAN
    near = scores - top
    factor_ref[0:heads, :] = jnp.exp(near)
    factor_ref[heads : 2 * heads, :] = jnp.exp(0.2 * near)

    perm = order_matrix(128, False)
    dst_hidden = jnp.concatenate(
        [
            dot(dot(perm, dst_ref[b * 128 : b * 128 + 128, :]).astype(BF), weight).astype(BF)
            for b in range(blocks)
        ],
        0,
    )
    d_ref[...] = dot_exact(dst_hidden, adst_ref[...])
    acc_ref[...] = jnp.zeros_like(acc_ref)
    for copy in copies:
        copy.wait()

    bit_row = jnp.left_shift(1, lax.broadcasted_iota(jnp.int32, (1, 1024), 1) % 8)

    def bits(q, bs):
        words = [mask_ref[pl.ds(inv_ref[b * nsb + q], 16, stride=pitch), :] for b in bs]
        words = jnp.concatenate(words, 0) if len(words) > 1 else words[0]
        spread = dot(words.astype(F32).astype(BF), expand_ref[...]).astype(jnp.int32)
        return jnp.where((spread & bit_row) != 0, 1.0, 0.0)

    def tile_of(flags, k):
        return jnp.concatenate([flags[16 * k : 16 * k + 16, 128 * r : 128 * r + 128] for r in range(8)], 0)

    @pl.when(jnp.logical_not(wide))
    def _():
        for h in range(heads):
            cols = slice(h * 128, h * 128 + 128)
            t = d_ref[:, cols] + top[h : h + 1, :]
            m = leaky(t)
            m_ref[:, cols] = m
            fa_ref[:, cols] = jnp.exp(t - m).astype(BF)
            fc_ref[:, cols] = jnp.exp(0.2 * t - m).astype(BF)

        def step(g, carry):
            for qq in range(GROUP):
                q = g * GROUP + qq
                flags = bits(q, range(blocks))
                tiles = [tile_of(flags, b).astype(BF).reshape(8, 16, 128) for b in range(blocks)]
                place = pl.ds(pl.multiple_of(q * 128, 128), 128)
                rows = factor_ref[:, place]
                for h in range(heads):
                    cols = slice(h * 128, h * 128 + 128)
                    fb = jnp.broadcast_to(rows[h : h + 1], (16, 128)).astype(BF)[None]
                    fd = jnp.broadcast_to(rows[heads + h : heads + h + 1], (16, 128)).astype(BF)[None]
                    for b in range(blocks):
                        rs = slice(b * 128, b * 128 + 128)
                        fa = fa_ref[rs, cols].reshape(8, 16, 128)
                        fc = fc_ref[rs, cols].reshape(8, 16, 128)
                        w = jnp.maximum(fa * fb, fc * fd) * tiles[b]
                        w_ref[h, rs, qq * 128 : qq * 128 + 128] = w.reshape(128, 128)
            span = pl.ds(pl.multiple_of(g * GROUP * 128, GROUP * 128), GROUP * 128)
            for h in range(heads):
                cols = slice(h * 128, h * 128 + 128)
                acc_ref[:, cols] += dot(w_ref[h], value_ref[span, cols])
            return carry

        lax.fori_loop(0, nsb // GROUP, step, 0)

    @pl.when(wide)
    def _():
        for b in range(blocks):
            rs = slice(b * 128, b * 128 + 128)
            for h in range(heads):
                cols = slice(h * 128, h * 128 + 128)

                def top_step(q, best):
                    flag = tile_of(bits(q, (b,)), 0) > 0.5
                    s = score_ref[h : h + 1, pl.ds(pl.multiple_of(q * 128, 128), 128)]
                    return jnp.maximum(best, jnp.where(flag, s, NEG))

                best = lax.fori_loop(0, nsb, top_step, jnp.full((128, 128), NEG, F32))
                d = d_ref[rs, cols]
                m = leaky(d + jnp.max(best, axis=1, keepdims=True))
                m_ref[rs, cols] = m

                def sum_step(q, total):
                    flag = tile_of(bits(q, (b,)), 0) > 0.5
                    place = pl.ds(pl.multiple_of(q * 128, 128), 128)
                    s = score_ref[h : h + 1, place]
                    w = jnp.where(flag, jnp.exp(leaky(d + s) - m), 0.0).astype(BF)
                    return total + dot(w, value_ref[place, cols])

                acc_ref[rs, cols] = lax.fori_loop(0, nsb, sum_step, jnp.zeros((128, 128), F32))

    back = order_matrix(128, True)
    for b in range(blocks):
        rs = slice(b * 128, b * 128 + 128)
        nums = []
        aux = jnp.zeros((128, 128), F32)
        for h in range(heads):
            cols = slice(h * 128, h * 128 + 128)
            acc = acc_ref[rs, cols]
            nums.append(acc)
            first, second, _ = (p.astype(F32) for p in split3(acc))
            base = 0 if h % 2 else half
            aux = jnp.where(lane == base + h, first, aux)
            aux = jnp.where(lane == base + 8 + h, second, aux)
            for k, part in enumerate(split3(m_ref[rs, cols])):
                aux = jnp.where(lane == 16 + 4 * k + h, part.astype(F32), aux)
        pairs = [jnp.where(lane < half, nums[2 * k], nums[2 * k + 1]) for k in range(heads // 2)]
        send = jnp.concatenate(pairs + [aux], 1).astype(BF)
        out_ref[rs, :] = dot(back, send).astype(BF)


def final_kernel(heads, peers, recv_ref, dst_ref, weight_ref, gsrc_ref, gdst_ref, out_ref):
    units = weight_ref.shape[1]
    half = units // heads
    own = dst_ref.shape[0]
    hidden = dot(dst_ref[...], weight_ref[...]).astype(BF)
    self_score = leaky(dot_exact(hidden, gdst_ref[...]) + dot_exact(hidden, gsrc_ref[...]))
    l = lax.broadcasted_iota(jnp.int32, (128, units), 0)
    h = lax.broadcasted_iota(jnp.int32, (128, units), 1) // half
    base = jnp.where(h % 2 == 1, 0, half)
    take_den = jnp.where((l == base + h) | (l == base + 8 + h), 1.0, 0.0).astype(BF)
    take_top = jnp.where((l == 16 + h) | (l == 20 + h) | (l == 24 + h), 1.0, 0.0).astype(BF)
    aux = recv_ref[:, units : units + 128]
    dens = dot(aux, take_den)
    tops = jnp.where(dens > 0, dot(aux, take_top), NEG)
    best = self_score
    for k in range(peers):
        best = jnp.maximum(best, tops[k * own : (k + 1) * own])
    self_weight = jnp.exp(self_score - best)
    den = self_weight
    num = self_weight.astype(BF).astype(F32) * hidden.astype(F32)
    for k in range(peers):
        rows = slice(k * own, (k + 1) * own)
        scale = jnp.exp(tops[rows] - best)
        den = den + dens[rows] * scale
        num = num + recv_ref[rows, 0:units].astype(F32) * scale
    out_ref[...] = (num / den).astype(BF)


def body(
    src_feats, dst_feats, proj_weight, attn_src, attn_dst, tile_dst, tile_src, tile_live, tile_mask
):
    heads, half = attn_src.shape
    units = heads * half
    peers = lax.axis_size("col")
    own = dst_feats.shape[0]
    nd = own * peers
    blocks = nd // 128
    slab = lax.all_gather(src_feats, "row", axis=0, tiled=True)
    dst_all = lax.all_gather(dst_feats, "col", axis=0, tiled=True)
    nsb = slab.shape[0] // 128
    slots = tile_mask.shape[1]
    pitch = slots + 8
    slot = jnp.arange(slots, dtype=jnp.int32)
    pair = jnp.where(slot < tile_live[0, 0], tile_dst[0] * nsb + tile_src[0], -1)
    hit = pair[None, :] == jnp.arange(blocks * nsb, dtype=jnp.int32)[:, None]
    inv = jnp.min(jnp.where(hit, slot[None, :], slots), axis=1)
    flat_src = attn_src.reshape(units)
    flat_dst = attn_dst.reshape(units)
    unit_head = jnp.arange(units) // half
    arows = jnp.where(jnp.arange(8)[:, None] == unit_head[None, :], flat_src[None, :], 0.0)
    acols = jnp.where(
        unit_head[:, None] == jnp.arange(heads * 128)[None, :] // 128, flat_dst[:, None], 0.0
    )
    same = unit_head[:, None] == unit_head[None, :]
    gsrc = jnp.where(same, flat_src[:, None], 0.0)
    gdst = jnp.where(same, flat_dst[:, None], 0.0)
    wide = jnp.arange(1024)
    expand = (
        jnp.arange(128)[:, None] == ((wide // 128) * 16 + (wide % 128) // 8)[None, :]
    ).astype(BF)
    vm = pl.BlockSpec(memory_space=pltpu.VMEM)
    send = pl.pallas_call(
        functools.partial(main_kernel, heads),
        out_shape=jax.ShapeDtypeStruct((nd, units + 128), BF),
        in_specs=[pl.BlockSpec(memory_space=pltpu.SMEM)] + [vm] * 6 + [pl.BlockSpec(memory_space=pl.ANY)],
        out_specs=vm,
        scratch_shapes=[
            pltpu.VMEM((16 * pitch, 128), jnp.int32),
            pltpu.VMEM((slab.shape[0], heads * 128), BF),
            pltpu.VMEM((8, slab.shape[0]), F32),
            pltpu.VMEM((8, slab.shape[0]), F32),
            pltpu.VMEM((nd, heads * 128), BF),
            pltpu.VMEM((nd, heads * 128), BF),
            pltpu.VMEM((nd, heads * 128), F32),
            pltpu.VMEM((nd, heads * 128), F32),
            pltpu.VMEM((heads, nd, GROUP * 128), BF),
            pltpu.VMEM((nd, heads * 128), F32),
            pltpu.SemaphoreType.DMA((16,)),
        ],
        compiler_params=pltpu.CompilerParams(vmem_limit_bytes=56 * 1024 * 1024),
    )(inv, slab, dst_all, proj_weight, arows, acols, expand, tile_mask[0])
    recv = lax.all_to_all(send, "col", split_axis=0, concat_axis=0, tiled=True)
    return pl.pallas_call(
        functools.partial(final_kernel, heads, peers),
        out_shape=jax.ShapeDtypeStruct((own, units), BF),
        in_specs=[vm] * 5,
        out_specs=vm,
    )(recv, dst_feats, proj_weight, gsrc, gdst)


def solution(mesh):
    placed = (
        P(("row", "col"), None),
        P(("row", "col"), None),
        P(),
        P(),
        P(),
        P("row", "col"),
        P("row", "col"),
        P("row", "col"),
        P("row", "col", None),
    )
    return jax.shard_map(
        body, mesh=mesh, in_specs=placed, out_specs=P(("row", "col"), None), check_vma=False
    )
```

time: 579 us -> 552 us (0.953)
  Pallas kernels: 0 us -> 474 us
  waiting for transfers between devices: 302 us -> 39.7 us
  local copies, waits for them, and re-layouts: 94.2 us -> 2.27 us
  other arithmetic: 76.6 us -> 4.73 us
  matrix products: 58.1 us -> 0 us
  blocking collectives: 27.6 us -> 12.4 us
    pallas_call x0 -> x2, Pallas kernels: none -> 474 us  [the longest x1 472 us: body(): pl.pallas_call(functools.partial(main_kernel, heads), out_shape=jax.Shape...]
    all_gather x2 -> x1, waiting for transfers between devices: 302 us -> 31.7 us  [body(): slab = lax.all_gather(src_feats, 'row', axis=0, tiled=True)]
    dot_general x30 -> x0, matrix products: 58.1 us -> none  [the longest x14 39 us: one_turn(): jnp.einsum('ghij,gjhd->gihd', weights.astype(jnp.bfloat16), values.reshap...]
    gather x28 -> x0, local copies, waits for them, and re-layouts: 42.6 us -> none  [one_turn(): values = jnp.take(value_table, turn_source, axis=0)]
    reduce_sum x72 -> x0, other arithmetic: 38.6 us -> none  [the longest x14 27.1 us: one_turn(): jnp.sum(weights, axis=3)[:, None]]
    dynamic_slice x42 -> x0, local copies, waits for them, and re-layouts: 20.7 us -> none  [the longest x14 11.8 us: one_turn(): turn_packed = lax.dynamic_slice_in_dim(packed_all, offset, tiles_turn, 0)]
    reduce_max x28 -> x0, other arithmetic: 19.7 us -> none  [the longest x14 18.3 us: one_turn(): tile_top = jnp.max(jnp.where(present, scores, neg_fill), axis=3)]
    all_gather x3 -> x1, blocking collectives: 27.6 us -> 12.4 us  [body(): dst_all = lax.all_gather(dst_feats, 'col', axis=0, tiled=True)]
  transfers between devices with their start and end apart: 2 -> 2, of which waited for: 2 -> 2; matrix products, arithmetic and copies ran while one was open for 0% -> 1% of each run, Pallas kernels for 0% -> 0%
where the time goes in v1:
time: 552 us; the launch traced here: 551 us
  Pallas kernels  474 us (86%)
  waiting for transfers between devices  39.7 us (7%)
  between operations  14.1 us (3%)
  blocking collectives  12.4 us (2%)
    pallas_call x1, Pallas kernels, body(): pl.pallas_call(functools.partial(main_kernel, heads), out_shape=jax.Shape...  472 us
    all_gather x1, waiting for transfers between devices, body(): slab = lax.all_gather(src_feats, 'row', axis=0, tiled=True)  31.7 us
    all_gather x1, blocking collectives, body(): dst_all = lax.all_gather(dst_feats, 'col', axis=0, tiled=True)  12.4 us
  transfers between devices with their start and end apart: 2, of which 2 were waited for; matrix products, arithmetic and copies ran while one was open for 1% of the time, Pallas kernels for 0%

profile of v1, /device:TPU:0, one launch (start us, length us, event | category | flops | bytes accessed | tf_op | source)
XLA Modules:
  0.0 551.2 jit_solution(8927424314055492594)
XLA Ops:
  6.5 0.0 all-gather.2.cloned.1.call-start
  6.5 0.7 all-gather.2.cloned.1.call-update
  7.9 0.8 broadcast_in_dim.79
  8.7 0.8 broadcast_in_dim.82
  9.4 12.4 %all_gather.7.dst_ref = bf16[512,128]{1,0:T(8,128)(2,1)} all-gather(bf16[64,128]{1,0:T(8,128)(2,1)} %dst_ref.1), channel_id=1, replica_groups=mesh['row'=4,'col'=8] {'col'}, dimensions={0}, use_global_device_ids=true | all-gather | bytes 147456 | tf_op jit(solution)/shard_map/all_gather | solution.py:240
  21.9 0.7 compare_select_fusion.3
  22.6 0.7 select_reduce_fusion.inv_ref
  23.3 0.6 fusion.5.asrc_ref
  23.9 0.8 fusion.expand_ref
  24.7 0.9 compare_select_fusion.adst_ref
  25.6 31.7 %all-gather.2.cloned.1.call-done.feats_ref = bf16[8192,128]{1,0:T(8,128)(2,1)} async-done(((bf16[2048,128]{1,0:T(8,128)(2,1)}), bf16[8192,128]{1,0:T(8,128)(2,1)}) %all-gather.2.cloned.1.call-update) | async-done | bytes 2097168 | tf_op jit(solution)/shard_map/all_gather | solution.py:239
  57.3 471.9 %shard_map.91 = bf16[512,384]{1,0:T(8,128)(2,1)} custom-call(s32[256]{0:T(256)} %select_reduce_fusion.inv_ref, bf16[8192,128]{1,0:T(8,128)(2,1)} %all-gather.2.cloned.1.call-done.feats_ref, bf16[512,128]{1,0:T(8,128)(2,1)} %all_gather.7.dst_ref, bf16[128,256]{1,0:T(8,128)(2,1)} %weight_ref.3, f32[8,256]{1,0:T(8,128)} %fusion.5.asrc_ref, ...), custom_call_target="tpu_custom_call" | custom-call | tf_op jit(solution)/shard_map/pallas_call | solution.py:263
  529.2 3.7 all-to-all-start
  532.9 1.0 compare_select_fusion.1
  533.9 7.3 %all-to-all-done = bf16[8,64,384]{2,1,0:T(8,128)(2,1)S(1)} async-done(((bf16[8,64,384]{2,1,0:T(8,128)(2,1)}), bf16[8,64,384]{2,1,0:T(8,128)(2,1)S(1)}, u32[]{:S(2)}, u32[]{:S(2)}) %all-to-all-start) | async-done | bytes 393248 | tf_op jit(solution)/shard_map/all_to_all | solution.py:283
  541.2 0.0 copy-start
  541.2 0.7 copy-done
  541.9 2.5 shard_map.92
  (3 shorter events, 0.0 us)
Async XLA Ops:
  6.5 50.8 %all-gather.2.cloned.1.call-start = ((), (), s32[]{:S(2)}) async-start(), calls=%async_computation.1 | async-start | bytes 2621440 | tf_op jit(solution)/shard_map/all_gather | solution.py:239
  529.2 12.0 %all-to-all-start = ((bf16[8,64,384]{2,1,0:T(8,128)(2,1)}), bf16[8,64,384]{2,1,0:T(8,128)(2,1)S(1)}, u32[]{:S(2)}, u32[]{:S(2)}) async-start(bf16[8,64,384]{2,1,0:T(8,128)(2,1)} %bitcast.7), calls=%async_computation | async-start | bytes 786432 | tf_op jit(solution)/shard_map/all_to_all | solution.py:283
  541.2 0.7 copy-start
Sparse Core Ops, SparseCore 0:
  8.9 48.3 all-gather.1

commit v2 on v1

--- a/solution.py
+++ b/solution.py
@@ -44,8 +44,7 @@
 
 def main_kernel(
     heads, inv_ref, feats_ref, dst_ref, weight_ref, asrc_ref, adst_ref, expand_ref, packed_ref,
-    out_ref, mask_ref, value_ref, score_ref, factor_ref, fa_ref, fc_ref, d_ref, m_ref, w_ref,
-    acc_ref, sems
+    out_ref, mask_ref, value_ref, score_ref, d_ref, m_ref, acc_ref, sems
 ):
     units = weight_ref.shape[1]
     slabs = feats_ref.shape[0]
@@ -86,14 +85,6 @@
         return carry
 
     lax.fori_loop(0, slabs // chunk, project, 0)
-    scores = score_ref[0:heads, :]
-    top = jnp.max(scores, axis=1, keepdims=True)
-    low = jnp.min(scores, axis=1, keepdims=True)
-    wide = jnp.max(top - low) > SPAN
-    near = scores - top
-    factor_ref[0:heads, :] = jnp.exp(near)
-    factor_ref[heads : 2 * heads, :] = jnp.exp(0.2 * near)
-
     perm = order_matrix(128, False)
     dst_hidden = jnp.concatenate(
         [
@@ -118,43 +109,7 @@
     def tile_of(flags, k):
         return jnp.concatenate([flags[16 * k : 16 * k + 16, 128 * r : 128 * r + 128] for r in range(8)], 0)
 
-    @pl.when(jnp.logical_not(wide))
-    def _():
-        for h in range(heads):
-            cols = slice(h * 128, h * 128 + 128)
-            t = d_ref[:, cols] + top[h : h + 1, :]
-            m = leaky(t)
-            m_ref[:, cols] = m
-            fa_ref[:, cols] = jnp.exp(t - m).astype(BF)
-            fc_ref[:, cols] = jnp.exp(0.2 * t - m).astype(BF)
-
-        def step(g, carry):
-            for qq in range(GROUP):
-                q = g * GROUP + qq
-                flags = bits(q, range(blocks))
-                tiles = [tile_of(flags, b).astype(BF).reshape(8, 16, 128) for b in range(blocks)]
-                place = pl.ds(pl.multiple_of(q * 128, 128), 128)
-                rows = factor_ref[:, place]
-                for h in range(heads):
-                    cols = slice(h * 128, h * 128 + 128)
-                    fb = jnp.broadcast_to(rows[h : h + 1], (16, 128)).astype(BF)[None]
-                    fd = jnp.broadcast_to(rows[heads + h : heads + h + 1], (16, 128)).astype(BF)[None]
-                    for b in range(blocks):
-                        rs = slice(b * 128, b * 128 + 128)
-                        fa = fa_ref[rs, cols].reshape(8, 16, 128)
-                        fc = fc_ref[rs, cols].reshape(8, 16, 128)
-                        w = jnp.maximum(fa * fb, fc * fd) * tiles[b]
-                        w_ref[h, rs, qq * 128 : qq * 128 + 128] = w.reshape(128, 128)
-            span = pl.ds(pl.multiple_of(g * GROUP * 128, GROUP * 128), GROUP * 128)
-            for h in range(heads):
-                cols = slice(h * 128, h * 128 + 128)
-                acc_ref[:, cols] += dot(w_ref[h], value_ref[span, cols])
-            return carry
-
-        lax.fori_loop(0, nsb // GROUP, step, 0)
-
-    @pl.when(wide)
-    def _():
+    if True:
         for b in range(blocks):
             rs = slice(b * 128, b * 128 + 128)
             for h in range(heads):
@@ -226,6 +181,315 @@
         num = num + recv_ref[rows, 0:units].astype(F32) * scale
     out_ref[...] = (num / den).astype(BF)
 
+def fused_kernel(
+    heads, rows_n, cols_n, inv_ref, feats_ref, own_dst_ref, weight_ref, asrc_ref, adst_ref,
+    expand_ref, gsrc_ref, gdst_ref, packed_ref, out_ref, flag_ref, mask_ref, slab_ref, dst_ref,
+    value_ref, score_ref, fa_ref, fc_ref, m_ref, w_ref, acc_ref, send_ref, recv_ref, mask_sems,
+    feat_send, feat_recv, dst_send, dst_recv, part_send, part_recv
+):
+    z = lax.axis_index("row")
+    c = lax.axis_index("col")
+    units = weight_ref.shape[1]
+    half = units // heads
+    shard = feats_ref.shape[0]
+    chunk = GROUP * 128
+    chunks = shard // chunk
+    nsb = rows_n * shard // 128
+    own = own_dst_ref.shape[0]
+    nd = own * cols_n
+    blocks = nd // 128
+    slots = packed_ref.shape[0]
+    pitch = mask_ref.shape[0] // 16
+    mesh_id = pl.DeviceIdType.MESH
+
+    mask_copies = [
+        pltpu.make_async_copy(
+            packed_ref.at[:, pl.ds(u * 128, 128)],
+            mask_ref.at[pl.ds(u * pitch, slots), :],
+            mask_sems.at[u],
+        )
+        for u in range(16)
+    ]
+    for copy in mask_copies:
+        copy.start()
+
+    barrier = pltpu.get_barrier_semaphore()
+
+    def greet_col(k, carry):
+        pl.semaphore_signal(
+            barrier, inc=1, device_id=(z, (c + k) % cols_n), device_id_type=mesh_id
+        )
+        return carry
+
+    lax.fori_loop(1, cols_n, greet_col, 0)
+
+    @pl.when(z > 0)
+    def _():
+        pl.semaphore_signal(barrier, inc=1, device_id=(z - 1, c), device_id_type=mesh_id)
+
+    @pl.when(z < rows_n - 1)
+    def _():
+        pl.semaphore_signal(barrier, inc=1, device_id=(z + 1, c), device_id_type=mesh_id)
+
+    beside = (z + rows_n - 1) // rows_n + (2 * rows_n - 2 - z) // rows_n
+    pl.semaphore_wait(barrier, cols_n - 1 + beside)
+
+    def feat_copy(src, o, ch, side):
+        return pltpu.make_async_remote_copy(
+            src_ref=src,
+            dst_ref=slab_ref.at[pl.ds(pl.multiple_of(o * shard + ch * chunk, chunk), chunk), :],
+            send_sem=feat_send.at[side, o * chunks + ch],
+            recv_sem=feat_recv.at[o * chunks + ch],
+            device_id=((z + 1 - 2 * side + rows_n) % rows_n, c),
+            device_id_type=mesh_id,
+        )
+
+    def slab_chunk(o, ch):
+        return slab_ref.at[pl.ds(pl.multiple_of(o * shard + ch * chunk, chunk), chunk), :]
+
+    def dst_copy(k, who):
+        return pltpu.make_async_remote_copy(
+            src_ref=own_dst_ref,
+            dst_ref=dst_ref.at[pl.ds(pl.multiple_of(who * own, own), own), :],
+            send_sem=dst_send.at[k],
+            recv_sem=dst_recv.at[k],
+            device_id=(z, (c + k) % cols_n),
+            device_id_type=mesh_id,
+        )
+
+    def send_dst(k, carry):
+        dst_copy(k, c).start()
+        return carry
+
+    lax.fori_loop(1, cols_n, send_dst, 0)
+
+    def send_own(ch, carry):
+        src = feats_ref.at[pl.ds(pl.multiple_of(ch * chunk, chunk), chunk), :]
+
+        @pl.when(z < rows_n - 1)
+        def _():
+            feat_copy(src, z, ch, 0).start()
+
+        @pl.when(z > 0)
+        def _():
+            feat_copy(src, z, ch, 1).start()
+
+        return carry
+
+    lax.fori_loop(0, chunks, send_own, 0)
+    dst_ref[pl.ds(pl.multiple_of(c * own, own), own), :] = own_dst_ref[...]
+    for u in range(16):
+        mask_ref[u * pitch + slots : (u + 1) * pitch, :] = jnp.zeros((pitch - slots, 128), jnp.int32)
+    acc_ref[...] = jnp.zeros_like(acc_ref)
+
+    lane = lax.broadcasted_iota(jnp.int32, (1, 128), 1)
+    weight = weight_ref[...]
+    arows = asrc_ref[...]
+    a_parts = jnp.concatenate(
+        [p.astype(F32) for p in split3(arows)] + [jnp.zeros_like(arows)], 0
+    ).astype(BF)
+
+    def project(x, rows):
+        hidden = dot(x, weight).astype(BF)
+        parts = lax.dot_general(
+            a_parts, hidden, (((1,), (1,)), ((), ())), preferred_element_type=F32
+        )
+        score_ref[:, rows] = parts[0:8] + parts[8:16] + parts[16:24]
+        for h in range(heads):
+            tile = hidden[:, (h // 2) * 128 : (h // 2) * 128 + 128]
+            mine = (lane >= half) if h % 2 else (lane < half)
+            value_ref[rows, h * 128 : h * 128 + 128] = jnp.where(
+                mine, tile.astype(F32), 1.0
+            ).astype(BF)
+
+    def project_own(ch, carry):
+        rows = pl.ds(pl.multiple_of(z * shard + ch * chunk, chunk), chunk)
+        project(feats_ref[pl.ds(pl.multiple_of(ch * chunk, chunk), chunk), :], rows)
+        return carry
+
+    lax.fori_loop(0, chunks, project_own, 0)
+    own_scores = score_ref[:, pl.ds(pl.multiple_of(z * shard, shard), shard)]
+    top = jnp.max(own_scores, axis=1, keepdims=True)
+
+    def wait_dst(k, carry):
+        dst_copy(k, (c + cols_n - k) % cols_n).wait_recv()
+        return carry
+
+    lax.fori_loop(1, cols_n, wait_dst, 0)
+    perm = order_matrix(128, False)
+    dst_hidden = jnp.concatenate(
+        [
+            dot(dot(perm, dst_ref[b * 128 : b * 128 + 128, :]).astype(BF), weight).astype(BF)
+            for b in range(blocks)
+        ],
+        0,
+    )
+    d_all = dot_exact(dst_hidden, adst_ref[...])
+    for h in range(heads):
+        cols = slice(h * 128, h * 128 + 128)
+        t = d_all[:, cols] + top[h : h + 1, :]
+        m = leaky(t)
+        m_ref[:, cols] = m
+        fa_ref[:, cols] = jnp.exp(t - m).astype(BF)
+        fc_ref[:, cols] = jnp.exp(0.2 * t - m).astype(BF)
+    for copy in mask_copies:
+        copy.wait()
+    bit_row = jnp.left_shift(1, lax.broadcasted_iota(jnp.int32, (1, 1024), 1) % 8)
+
+    def step(g):
+        span = pl.ds(pl.multiple_of(g * chunk, chunk), chunk)
+        near = score_ref[0:8, span] - top
+        near_b = jnp.exp(near)
+        near_d = jnp.exp(0.2 * near)
+        for qq in range(GROUP):
+            q = g * GROUP + qq
+            words = jnp.concatenate(
+                [mask_ref[pl.ds(inv_ref[b * nsb + q], 16, stride=pitch), :] for b in range(blocks)], 0
+            )
+            spread = dot(words.astype(F32).astype(BF), expand_ref[...]).astype(jnp.int32)
+            flags = jnp.where((spread & bit_row) != 0, 1.0, 0.0)
+            tiles = [
+                jnp.concatenate(
+                    [flags[16 * b : 16 * b + 16, 128 * r : 128 * r + 128] for r in range(8)], 0
+                ).astype(BF).reshape(8, 16, 128)
+                for b in range(blocks)
+            ]
+            place = slice(qq * 128, qq * 128 + 128)
+            for h in range(heads):
+                cols = slice(h * 128, h * 128 + 128)
+                fb = jnp.broadcast_to(near_b[h : h + 1, place], (16, 128)).astype(BF)[None]
+                fd = jnp.broadcast_to(near_d[h : h + 1, place], (16, 128)).astype(BF)[None]
+                for b in range(blocks):
+                    rs = slice(b * 128, b * 128 + 128)
+                    fa = fa_ref[rs, cols].reshape(8, 16, 128)
+                    fc = fc_ref[rs, cols].reshape(8, 16, 128)
+                    w = jnp.maximum(fa * fb, fc * fd) * tiles[b]
+                    w_ref[h, rs, place] = w.reshape(128, 128)
+        for h in range(heads):
+            cols = slice(h * 128, h * 128 + 128)
+            acc_ref[:, cols] += dot(w_ref[h], value_ref[span, cols])
+
+    above = rows_n - 1 - z
+    both = jnp.minimum(z, above)
+    longer = jnp.where(above > z, 1, 0)
+    paired = 2 * both * chunks
+
+    def arrival(k):
+        first = k < paired
+        late = k - paired
+        hop = jnp.where(first, k // (2 * chunks), both + late // chunks) + 1
+        ch = jnp.where(first, (k % (2 * chunks)) // 2, (late + paired) % chunks)
+        side = jnp.where(first, k % 2, longer)
+        return jnp.where(side == 0, z - hop, z + hop), ch, side
+
+    def take(k):
+        o, ch, side = arrival(k)
+        feat_copy(slab_chunk(o, ch), o, ch, side).wait_recv()
+
+        @pl.when(jnp.where(side == 0, z < rows_n - 1, z > 0))
+        def _():
+            feat_copy(slab_chunk(o, ch), o, ch, side).start()
+
+    def turn(k, carry):
+        @pl.when(k >= chunks)
+        def _():
+            j = k - chunks
+            take(j)
+            o, ch, _ = arrival(j)
+            rows = pl.ds(pl.multiple_of(o * shard + ch * chunk, chunk), chunk)
+            project(slab_ref[rows, :], rows)
+
+        o, ch, _ = arrival(jnp.maximum(k - chunks, 0))
+        mine = k < chunks
+        step(jnp.where(mine, z * chunks + k, o * chunks + ch))
+        return carry
+
+    lax.fori_loop(0, rows_n * chunks, turn, 0)
+
+    scores = score_ref[0:heads, :]
+    spread_of = jnp.max(scores, axis=1, keepdims=True) - jnp.min(scores, axis=1, keepdims=True)
+    wide = jnp.where(jnp.max(spread_of, axis=0, keepdims=True) <= SPAN, 0.0, 1.0)
+    back = order_matrix(128, True)
+    for b in range(blocks):
+        rs = slice(b * 128, b * 128 + 128)
+        nums = []
+        aux = jnp.where(lane == 40, wide, jnp.zeros((128, 128), F32))
+        for h in range(heads):
+            cols = slice(h * 128, h * 128 + 128)
+            acc = acc_ref[rs, cols]
+            nums.append(acc)
+            first, second, _ = (p.astype(F32) for p in split3(acc))
+            base = 0 if h % 2 else half
+            aux = jnp.where(lane == base + h, first, aux)
+            aux = jnp.where(lane == base + 8 + h, second, aux)
+            for k, part in enumerate(split3(m_ref[rs, cols])):
+                aux = jnp.where(lane == 16 + 4 * k + h, part.astype(F32), aux)
+        pairs = [jnp.where(lane < half, nums[2 * k], nums[2 * k + 1]) for k in range(heads // 2)]
+        send = jnp.concatenate(pairs + [aux], 1).astype(BF)
+        send_ref[rs, :] = dot(back, send).astype(BF)
+
+    def part_copy(k, to, who):
+        return pltpu.make_async_remote_copy(
+            src_ref=send_ref.at[pl.ds(pl.multiple_of(to * own, own), own), :],
+            dst_ref=recv_ref.at[pl.ds(pl.multiple_of(who * own, own), own), :],
+            send_sem=part_send.at[k],
+            recv_sem=part_recv.at[k],
+            device_id=(z, (c + k) % cols_n),
+            device_id_type=mesh_id,
+        )
+
+    def send_part(k, carry):
+        part_copy(k, (c + k) % cols_n, c).start()
+        return carry
+
+    lax.fori_loop(1, cols_n, send_part, 0)
+    mine = pl.ds(pl.multiple_of(c * own, own), own)
+    recv_ref[mine, :] = send_ref[mine, :]
+
+    def end_part(k, carry):
+        part_copy(k, (c + k) % cols_n, (c + cols_n - k) % cols_n).wait_recv()
+        return carry
+
+    lax.fori_loop(1, cols_n, end_part, 0)
+    final_kernel(heads, cols_n, recv_ref, own_dst_ref, weight_ref, gsrc_ref, gdst_ref, out_ref)
+    seen = jnp.max(recv_ref[:, units : units + 128].astype(F32), axis=0, keepdims=True)
+    flag_ref[...] = jnp.broadcast_to(
+        jnp.max(jnp.where(lane == 40, seen, 0.0), axis=1, keepdims=True), flag_ref.shape
+    )
+
+    def end_send(k, carry):
+        part_copy(k, (c + k) % cols_n, c).wait_send()
+        dst_copy(k, c).wait_send()
+        return carry
+
+    lax.fori_loop(1, cols_n, end_send, 0)
+
+    def end_own(ch, carry):
+        src = feats_ref.at[pl.ds(pl.multiple_of(ch * chunk, chunk), chunk), :]
+
+        @pl.when(z < rows_n - 1)
+        def _():
+            feat_copy(src, z, ch, 0).wait_send()
+
+        @pl.when(z > 0)
+        def _():
+            feat_copy(src, z, ch, 1).wait_send()
+
+        return carry
+
+    lax.fori_loop(0, chunks, end_own, 0)
+
+    def end_relay(k, carry):
+        o, ch, side = arrival(k)
+
+        @pl.when(jnp.where(side == 0, z < rows_n - 1, z > 0))
+        def _():
+            feat_copy(slab_chunk(o, ch), o, ch, side).wait_send()
+
+        return carry
+
+    lax.fori_loop(0, (rows_n - 1) * chunks, end_relay, 0)
+
 
 def body(
     src_feats, dst_feats, proj_weight, attn_src, attn_dst, tile_dst, tile_src, tile_live, tile_mask
@@ -236,9 +500,10 @@
     own = dst_feats.shape[0]
     nd = own * peers
     blocks = nd // 128
-    slab = lax.all_gather(src_feats, "row", axis=0, tiled=True)
-    dst_all = lax.all_gather(dst_feats, "col", axis=0, tiled=True)
-    nsb = slab.shape[0] // 128
+    rows_n = lax.axis_size("row")
+    shard = src_feats.shape[0]
+    sources = shard * rows_n
+    nsb = sources // 128
     slots = tile_mask.shape[1]
     pitch = slots + 8
     slot = jnp.arange(slots, dtype=jnp.int32)
@@ -260,33 +525,75 @@
         jnp.arange(128)[:, None] == ((wide // 128) * 16 + (wide % 128) // 8)[None, :]
     ).astype(BF)
     vm = pl.BlockSpec(memory_space=pltpu.VMEM)
-    send = pl.pallas_call(
-        functools.partial(main_kernel, heads),
-        out_shape=jax.ShapeDtypeStruct((nd, units + 128), BF),
-        in_specs=[pl.BlockSpec(memory_space=pltpu.SMEM)] + [vm] * 6 + [pl.BlockSpec(memory_space=pl.ANY)],
-        out_specs=vm,
+    chunks = shard // (GROUP * 128)
+    fast, flag = pl.pallas_call(
+        functools.partial(fused_kernel, heads, rows_n, peers),
+        out_shape=(
+            jax.ShapeDtypeStruct((own, units), BF),
+            jax.ShapeDtypeStruct((8, 128), F32),
+        ),
+        in_specs=[pl.BlockSpec(memory_space=pltpu.SMEM)] + [vm] * 8 + [pl.BlockSpec(memory_space=pl.ANY)],
+        out_specs=(vm, vm),
         scratch_shapes=[
             pltpu.VMEM((16 * pitch, 128), jnp.int32),
-            pltpu.VMEM((slab.shape[0], heads * 128), BF),
-            pltpu.VMEM((8, slab.shape[0]), F32),
-            pltpu.VMEM((8, slab.shape[0]), F32),
+            pltpu.VMEM((sources, src_feats.shape[1]), BF),
+            pltpu.VMEM((nd, src_feats.shape[1]), BF),
+            pltpu.VMEM((sources, heads * 128), BF),
+            pltpu.VMEM((8, sources), F32),
             pltpu.VMEM((nd, heads * 128), BF),
             pltpu.VMEM((nd, heads * 128), BF),
             pltpu.VMEM((nd, heads * 128), F32),
-            pltpu.VMEM((nd, heads * 128), F32),
             pltpu.VMEM((heads, nd, GROUP * 128), BF),
             pltpu.VMEM((nd, heads * 128), F32),
+            pltpu.VMEM((nd, units + 128), BF),
+            pltpu.VMEM((nd, units + 128), BF),
             pltpu.SemaphoreType.DMA((16,)),
+            pltpu.SemaphoreType.DMA((2, rows_n * chunks)),
+            pltpu.SemaphoreType.DMA((rows_n * chunks,)),
+            pltpu.SemaphoreType.DMA((peers,)),
+            pltpu.SemaphoreType.DMA((peers,)),
+            pltpu.SemaphoreType.DMA((peers,)),
+            pltpu.SemaphoreType.DMA((peers,)),
         ],
-        compiler_params=pltpu.CompilerParams(vmem_limit_bytes=56 * 1024 * 1024),
-    )(inv, slab, dst_all, proj_weight, arows, acols, expand, tile_mask[0])
-    recv = lax.all_to_all(send, "col", split_axis=0, concat_axis=0, tiled=True)
-    return pl.pallas_call(
-        functools.partial(final_kernel, heads, peers),
-        out_shape=jax.ShapeDtypeStruct((own, units), BF),
-        in_specs=[vm] * 5,
-        out_specs=vm,
-    )(recv, dst_feats, proj_weight, gsrc, gdst)
+        compiler_params=pltpu.CompilerParams(
+            vmem_limit_bytes=56 * 1024 * 1024, collective_id=0, has_side_effects=True
+        ),
+    )(inv, src_feats, dst_feats, proj_weight, arows, acols, expand, gsrc, gdst, tile_mask[0])
+
+    def gathered(part, axis, count):
+        copies = jnp.broadcast_to(part[None], (count,) + part.shape)
+        return lax.all_to_all(copies, axis, 0, 0).reshape(count * part.shape[0], part.shape[1])
+
+    def general(_):
+        slab = gathered(src_feats, "row", rows_n)
+        dst_all = gathered(dst_feats, "col", peers)
+        send = pl.pallas_call(
+            functools.partial(main_kernel, heads),
+            out_shape=jax.ShapeDtypeStruct((nd, units + 128), BF),
+            in_specs=[pl.BlockSpec(memory_space=pltpu.SMEM)]
+            + [vm] * 6
+            + [pl.BlockSpec(memory_space=pl.ANY)],
+            out_specs=vm,
+            scratch_shapes=[
+                pltpu.VMEM((16 * pitch, 128), jnp.int32),
+                pltpu.VMEM((sources, heads * 128), BF),
+                pltpu.VMEM((8, sources), F32),
+                pltpu.VMEM((nd, heads * 128), F32),
+                pltpu.VMEM((nd, heads * 128), F32),
+                pltpu.VMEM((nd, heads * 128), F32),
+                pltpu.SemaphoreType.DMA((16,)),
+            ],
+            compiler_params=pltpu.CompilerParams(vmem_limit_bytes=56 * 1024 * 1024),
+        )(inv, slab, dst_all, proj_weight, arows, acols, expand, tile_mask[0])
+        recv = lax.all_to_all(send, "col", split_axis=0, concat_axis=0, tiled=True)
+        return pl.pallas_call(
+            functools.partial(final_kernel, heads, peers),
+            out_shape=jax.ShapeDtypeStruct((own, units), BF),
+            in_specs=[vm] * 5,
+            out_specs=vm,
+        )(recv, dst_feats, proj_weight, gsrc, gdst)
+
+    return lax.cond(flag[0, 0] > 0, general, lambda kept: kept, fast)
 
 
 def solution(mesh):

time: 552 us -> 610 us (1.11)
  blocking collectives: 12.4 us -> 72.4 us
  Pallas kernels: 474 us -> 531 us
  waiting for transfers between devices: 39.7 us -> 0 us
  between operations: 14.1 us -> 1.42 us
    all_to_all x0 -> x3, blocking collectives: none -> 72.4 us  [the longest x2 60 us: gathered(): lax.all_to_all(copies, axis, 0, 0)]
    pallas_call x2 -> x3, Pallas kernels: 474 us -> 531 us  [the longest x1 472 us: general(): pl.pallas_call(functools.partial(main_kernel, heads), out_shape=jax.Shape...]
    all_gather x1 -> x0, waiting for transfers between devices: 31.7 us -> none  [body(): slab = lax.all_gather(src_feats, 'row', axis=0, tiled=True)]
    all_gather x1 -> x0, blocking collectives: 12.4 us -> none  [body(): dst_all = lax.all_gather(dst_feats, 'col', axis=0, tiled=True)]
    all_to_all x1 -> x0, waiting for transfers between devices: 7.32 us -> none  [body(): recv = lax.all_to_all(send, 'col', split_axis=0, concat_axis=0, tiled=True)]
  transfers between devices with their start and end apart: 2 -> 0, of which waited for: 2 -> 0; matrix products, arithmetic and copies ran while one was open for 1% -> 0% of each run, Pallas kernels for 0% -> 0%
where the time goes in v2:
time: 610 us; the launch traced here: 609 us
  Pallas kernels  531 us (87%)
  blocking collectives  72.4 us (12%)
    pallas_call x1, Pallas kernels, general(): pl.pallas_call(functools.partial(main_kernel, heads), out_shape=jax.Shape...  472 us
    all_to_all x2, blocking collectives, gathered(): lax.all_to_all(copies, axis, 0, 0)  60 us
    pallas_call x1, Pallas kernels, body(): pl.pallas_call(functools.partial(fused_kernel, heads, rows_n, peers), out...  57.4 us
    all_to_all x1, blocking collectives, general(): recv = lax.all_to_all(send, 'col', split_axis=0, concat_axis=0, tiled=True)  12.4 us

profile of v2, /device:TPU:0, one launch (start us, length us, event | category | flops | bytes accessed | tf_op | source)
XLA Modules:
  0.0 609.5 jit_solution(16979632672438640355)
XLA Ops:
  0.7 0.7 compare_select_fusion.3
  1.4 0.1 select_reduce_fusion.inv_ref
  1.5 0.8 broadcast_in_dim.91
  2.2 0.8 broadcast_in_dim.94
  3.0 0.1 compare_select_fusion.adst_ref
  3.2 0.1 fusion.expand_ref
  3.2 0.2 compare_select_fusion.1
  3.4 0.0 copy-start
  3.4 0.0 copy-start.1
  3.4 0.0 copy-start.2
  3.4 0.0 copy-start.3
  3.5 57.4 %shard_map.93 = (bf16[64,256]{1,0:T(8,128)(2,1)S(1)}, f32[8,128]{1,0:T(8,128)}) custom-call(s32[256]{0:T(256)S(1)} %select_reduce_fusion.inv_ref, bf16[2048,128]{1,0:T(8,128)(2,1)} %feats_ref.1, bf16[64,128]{1,0:T(8,128)(2,1)} %own_dst_ref.1, bf16[128,256]{1,0:T(8,128)(2,1)} %weight_ref.1, f32[8,256]{1,0:T(8,128)S(1)} %fusion.5.asrc_ref, ...), custom_call_target="tpu_custom_call" | custom-call | tf_op jit(solution)/shard_map/pallas_call | solution.py:529
  60.8 1.2 slice.3
  62.7 0.0 copy-done
  62.7 0.0 copy-done.1
  62.7 0.0 copy-done.2
  62.7 546.1 %conditional.1 = (bf16[64,256]{1,0:T(8,128)(2,1)S(1)}) conditional(s32[]{:T(128)} %bitcast.8, bf16[64,256]{1,0:T(8,128)(2,1)S(1)} %get-tuple-element.42, (bf16[2048,128]{1,0:T(8,128)(2,1)S(1)}, bf16[64,128]{1,0:T(8,128)(2,1)S(1)}, s32[1,256,2048]{2,1,0:T(8,128)S(1)}, s32[256]{0:T(256)S(1)}, bf16[128,256]{1,0:T(8,128)(2,1)S(1)}, ...), branch_computations={%region_1.2_spmd, %region_2.3_spmd} | conditional | bytes 8011784 | solution.py:596
  62.8 8.6 %all_to_all.16 = bf16[8,64,128]{2,1,0:T(8,128)(2,1)} all-to-all(bf16[8,64,128]{2,1,0:T(8,128)(2,1)S(1)} %broadcast_in_dim.73), channel_id=1, replica_groups=mesh['row'=4,'col'=8] {'col'}, dimensions={0} | all-to-all | bytes 262144 | tf_op jit(solution)/shard_map/cond/branch_1_fun/all_to_all | solution.py:565
  71.3 0.3 broadcast_in_dim.72
  71.6 51.4 %all_to_all.17 = bf16[4,2048,128]{2,1,0:T(8,128)(2,1)} all-to-all(bf16[4,2048,128]{2,1,0:T(8,128)(2,1)S(1)} %broadcast_in_dim.72), channel_id=1, replica_groups=mesh['row'=4,'col'=8] {'row'}, dimensions={0} | all-to-all | bytes 4194304 | tf_op jit(solution)/shard_map/cond/branch_1_fun/all_to_all | solution.py:565
  123.0 471.8 %branch_1_fun.2 = bf16[512,384]{1,0:T(8,128)(2,1)} custom-call(s32[256]{0:T(256)S(1)} %get-tuple-element.29.inv_ref, bf16[8192,128]{1,0:T(8,128)(2,1)} %bitcast.12, bf16[512,128]{1,0:T(8,128)(2,1)} %bitcast.15, bf16[128,256]{1,0:T(8,128)(2,1)S(1)} %get-tuple-element.32.weight_ref, f32[8,256]{1,0:T(8,128)S(1)} %get-tuple-element.33.asrc_ref, ...), custom_call_target="tpu_custom_call" | custom-call | tf_op jit(solution)/shard_map/cond/branch_1_fun/pallas_call | solution.py:570
  594.8 12.4 %all_to_all.18 = bf16[8,64,384]{2,1,0:T(8,128)(2,1)} all-to-all(bf16[8,64,384]{2,1,0:T(8,128)(2,1)} %bitcast.13), channel_id=1, replica_groups=mesh['row'=4,'col'=8] {'col'}, dimensions={0} | all-to-all | bytes 786432 | tf_op jit(solution)/shard_map/cond/branch_1_fun/all_to_all | solution.py:588
  607.2 1.7 branch_1_fun.3
  608.9 0.6 copy.16
  (6 shorter events, 0.0 us)
Async XLA Ops:
  3.4 59.3 %copy-start = (s32[1,256,2048]{2,1,0:T(8,128)S(1)}, s32[1,256,2048]{2,1,0:T(8,128)}, u32[]{:S(2)}) copy-start(s32[1,256,2048]{2,1,0:T(8,128)} %param.19) | copy-start | bytes 6291460
  3.4 59.3 %copy-start.1 = (bf16[2048,128]{1,0:T(8,128)(2,1)S(1)}, bf16[2048,128]{1,0:T(8,128)(2,1)}, u32[]{:S(2)}) copy-start(bf16[2048,128]{1,0:T(8,128)(2,1)} %feats_ref.1) | copy-start | bytes 1572868
  3.4 59.3 %copy-start.2 = (bf16[128,256]{1,0:T(8,128)(2,1)S(1)}, bf16[128,256]{1,0:T(8,128)(2,1)}, u32[]{:S(2)}) copy-start(bf16[128,256]{1,0:T(8,128)(2,1)} %weight_ref.1) | copy-start | bytes 196612
  3.4 59.3 %copy-start.3 = (bf16[64,128]{1,0:T(8,128)(2,1)S(1)}, bf16[64,128]{1,0:T(8,128)(2,1)}, u32[]{:S(2)}) copy-start(bf16[64,128]{1,0:T(8,128)(2,1)} %own_dst_ref.1) | copy-start | bytes 49156
